TPU v7x, 32 devices: a whole 2x2x4 slice. The times are simulated.
32 devices in a mesh: groups: 2 (over x), tm: 16 (over z, y, core).
Axes of the slice: x: 2, y: 2, z: 4, core: 2. Of those that a mesh axis runs over, the one named last changes fastest.
Arguments:
- pixels: bfloat16 [128, 128, 1536], P(('groups', 'tm')), parts along dimension 0, as said below
- prior_kv: bfloat16 [2, 16, 128, 640], P(None, 'groups'), parts along dimension 1, may hold values from -6 to 6
- w_embed: bfloat16 [1536, 1280], replicated, may hold values from -0.15625 to 0.15625
- ln_gain: float32 [1280], replicated, may hold values from 0.1 to 1.9
- w_query: bfloat16 [1280, 640], replicated, as said below
- w_key: bfloat16 [1280, 640], replicated, as said below
- w_value: bfloat16 [1280, 640], replicated, may hold values from -0.15625 to 0.15625
- w_out: bfloat16 [640, 1280], replicated, may hold values from -0.25 to 0.25
Outputs:
- encoded: bfloat16 [128, 128, 1280], P(('groups', 'tm')), parts along dimension 0
There are 2 independent parts, one for each index of `groups`. A program takes and returns all parts, laid end to end along the dimension named above; an argument that names none is the same for every part. Nothing has to cross between parts.
Inputs may be any that keep to these rules, and one draw needn't show every extreme that they name: `pixels`: standardized pixel values. `w_query`: query projection, entries of order 1280 ** -0.5. `w_key`: key projection.
All inputs are finite; a program needn't handle non-finite values.
Results may differ from a plain program's by a relative error of at most 0.007.
Values may be sent and summed in bfloat16 or wider, within the bound.
A program may use at most 64 MiB of HBM per device.

v0:
```python
import math

import jax
import jax.numpy as jnp
from jax import lax
from jax.sharding import PartitionSpec as P

HEADS = 8
HEAD_DIM = 80


def shifted_2(value, axis, steps):
    count = lax.axis_size(axis)
    first, last = (max(0, -steps), min(count, count - steps))
    return lax.ppermute(value, axis, [(source, source + steps) for source in range(first, last)])


def body(pixels, prior_kv, w_embed, ln_gain, w_query, w_key, w_value, w_out):
    tub, pat, pix = pixels.shape
    width = w_embed.shape[1]
    flat = pixels.reshape(tub * pat, pix)
    embedded = jnp.dot(flat, w_embed, preferred_element_type=jnp.float32).astype(jnp.bfloat16)
    e_wide = embedded.astype(jnp.float32)
    center = e_wide - jnp.mean(e_wide, axis=-1, keepdims=True)
    spread = jnp.mean(center * center, axis=-1, keepdims=True)
    normed = (center * lax.rsqrt(spread + 1e-06) * ln_gain).astype(jnp.bfloat16)
    shape4 = (tub, pat, HEADS, HEAD_DIM)
    query = (
        jnp.dot(normed, w_query, preferred_element_type=jnp.float32)
        .astype(jnp.bfloat16)
        .reshape(shape4)
    )
    key = (
        jnp.dot(normed, w_key, preferred_element_type=jnp.float32)
        .astype(jnp.bfloat16)
        .reshape(shape4)
    )
    value = (
        jnp.dot(normed, w_value, preferred_element_type=jnp.float32)
        .astype(jnp.bfloat16)
        .reshape(shape4)
    )
    prior_key = prior_kv[0].reshape(2 * tub, pat, HEADS, HEAD_DIM)
    prior_value = prior_kv[1].reshape(2 * tub, pat, HEADS, HEAD_DIM)
    position = lax.axis_index("tm")
    is_first = position == 0
    near_raw = shifted_2((key, value), "tm", 1)
    near_key = jnp.where(is_first, prior_key[tub:], near_raw[0])
    near_value = jnp.where(is_first, prior_value[tub:], near_raw[1])
    far_raw = shifted_2((near_key, near_value), "tm", 1)
    far_key = jnp.where(is_first, prior_key[:tub], far_raw[0])
    far_value = jnp.where(is_first, prior_value[:tub], far_raw[1])
    keys_all = jnp.concatenate([far_key, near_key, key], axis=0)
    values_all = jnp.concatenate([far_value, near_value, value], axis=0)
    scale = 1.0 / math.sqrt(HEAD_DIM)
    reach = 2 * tub
    score_list = []
    for offset in range(reach + 1):
        shifted = lax.slice_in_dim(keys_all, reach - offset, reach - offset + tub, axis=0)
        score_list.append(
            jnp.einsum("tphe,tphe->thp", query, shifted, preferred_element_type=jnp.float32) * scale
        )
    scores = jnp.stack(score_list, axis=0)
    top = jnp.max(scores, axis=0, keepdims=True)
    expo = jnp.exp(scores - top)
    weights = (expo / jnp.sum(expo, axis=0, keepdims=True)).astype(jnp.bfloat16)
    mixed = jnp.zeros(shape4, jnp.float32)
    for offset in range(reach + 1):
        shifted = lax.slice_in_dim(values_all, reach - offset, reach - offset + tub, axis=0)
        mixed = mixed + jnp.einsum(
            "thp,tphe->tphe", weights[offset], shifted, preferred_element_type=jnp.float32
        )
    mixed = mixed.astype(jnp.bfloat16).reshape(tub * pat, HEADS * HEAD_DIM)
    encoded = e_wide + jnp.dot(mixed, w_out, preferred_element_type=jnp.float32)
    return encoded.astype(jnp.bfloat16).reshape(tub, pat, width)


def solution(mesh):
    placed = (
        P(("groups", "tm"), None, None),
        P(None, "groups", None, None),
        P(),
        P(),
        P(),
        P(),
        P(),
        P(),
    )
    return jax.shard_map(
        body, mesh=mesh, in_specs=placed, out_specs=P(("groups", "tm"), None, None), check_vma=False
    )
```

profile of v0, /device:TPU:1, one launch (start us, length us, event | category | flops | bytes accessed | tf_op | source)
XLA Modules:
  0.0 69.2 jit_solution(10895523290927638462)
XLA Ops:
  0.0 5.0 %convert_reduce_fusion = (f32[512]{0:T(512)S(1)}, bf16[512,1280]{1,0:T(8,128)(2,1)S(1)}) fusion(bf16[512,1536]{1,0:T(8,128)(2,1)} %bitcast.159, bf16[1536,1280]{1,0:T(8,128)(2,1)} %param.10), kind=kOutput, calls=%fused_computation.11 | convolution fusion | flops 2015231488 | bytes 6817792 | tf_op jit(solution)/shard_map/dot_general | solution.py:22
  5.5 0.5 copy-done.3
  6.1 1.3 %convolution_convert_fusion.2 = bf16[512,640]{1,0:T(8,128)(2,1)S(1)} fusion(bf16[1280,640]{1,0:T(8,128)(2,1)S(1)} %copy-done.5, bf16[512,1280]{1,0:T(8,128)(2,1)S(1)} %get-tuple-element.31, f32[1280]{0:T(1024)S(1)} %copy-done.6, f32[512]{0:T(512)S(1)} %add_rsqrt_fusion, f32[512]{0:T(512)S(1)} %broadcast_multiply_fusion), kind=kOutput, calls=%fused_computation.36 | convolution fusion | flops 842465280 | bytes 3613696 | tf_op jit(solution)/shard_map/dot_general | solution.py:34
  7.7 1.0 %reshape.110 = bf16[4,128,8,80]{1,0,3,2:T(4,128)(2,1)} reshape(bf16[512,640]{0,1:T(8,128)(2,1)S(1)} %copy.10) | data formatting | bytes 1310720 | tf_op jit(solution)/shard_map/reshape | solution.py:36
  8.7 4.5 %collective-permute-start = (bf16[4,128,8,80]{1,0,3,2:T(4,128)(2,1)}, bf16[4,128,8,80]{1,0,3,2:T(4,128)(2,1)}, u32[]{:S(2)}, u32[]{:S(2)}) collective-permute-start(bf16[4,128,8,80]{1,0,3,2:T(4,128)(2,1)} %reshape.110), channel_id=1, source_target_pairs={{0,1},{1,2},{2,3},{3,4},{4,5},{5,6},{6,7},{7,8},{8,9},{9,10},{10,1... | collective-permute-start | bytes 1966088 | tf_op jit(solution)/shard_map/ppermute | solution.py:15
  13.2 3.1 %convolution_convert_fusion.1 = bf16[512,640]{1,0:T(8,128)(2,1)S(1)} fusion(bf16[1280,640]{1,0:T(8,128)(2,1)} %param.14, bf16[512,1280]{1,0:T(8,128)(2,1)} %copy-done.3, f32[1280]{0:T(1024)S(1)} %copy-done.6, f32[512]{0:T(512)S(1)} %add_rsqrt_fusion, f32[512]{0:T(512)S(1)} %broadcast_multiply_fusion), kind=kOutput, calls=%fused_computation.35 | convolution fusion | flops 842465280 | bytes 3613696 | tf_op jit(solution)/shard_map/dot_general | solution.py:39
  16.6 1.0 %reshape.112 = bf16[4,128,8,80]{1,0,3,2:T(4,128)(2,1)} reshape(bf16[512,640]{0,1:T(8,128)(2,1)S(1)} %copy.15) | data formatting | bytes 1310720 | tf_op jit(solution)/shard_map/reshape | solution.py:41
  17.6 1.9 %collective-permute-start.2 = (bf16[4,128,8,80]{1,0,3,2:T(4,128)(2,1)}, bf16[4,128,8,80]{1,0,3,2:T(4,128)(2,1)}, u32[]{:S(2)}, u32[]{:S(2)}) collective-permute-start(bf16[4,128,8,80]{1,0,3,2:T(4,128)(2,1)} %reshape.112), channel_id=1, source_target_pairs={{0,1},{1,2},{2,3},{3,4},{4,5},{5,6},{6,7},{7,8},{8,9},{9,10},{10,1... | collective-permute-start | bytes 1966088 | tf_op jit(solution)/shard_map/ppermute | solution.py:15
  19.5 3.1 %fusion.35 = (bf16[1,4,128,640]{3,2,1,0:T(8,128)(2,1)}, bf16[1,4,128,640]{3,2,1,0:T(8,128)(2,1)S(1)}, bf16[1,4,128,640]{3,2,1,0:T(8,128)(2,1)}, bf16[1,4,128,640]{3,2,1,0:T(8,128)(2,1)S(1)}) fusion(bf16[2,8,128,640]{3,2,1,0:T(8,128)(2,1)} %param.9), kind=kLoop, calls=%fused_computation.105 | loop fusion | bytes 5242880 | tf_op jit(solution)/shard_map/slice | solution.py:51
  22.5 2.2 %copy.83 = bf16[1,4,128,640]{2,3,1,0:T(8,128)(2,1)} copy(bf16[1,4,128,640]{3,2,1,0:T(8,128)(2,1)} %get-tuple-element.19) | data formatting | bytes 1310720
  24.7 2.8 %copy_select_fusion.3 = bf16[4,128,8,80]{1,0,3,2:T(4,128)(2,1)} fusion(bf16[4,128,8,80]{1,0,3,2:T(4,128)(2,1)} %collective-permute-done, bf16[4,128,8,80]{1,3,2,0:T(8,128)(2,1)} %bitcast.156, pred[]{:T(512)S(6)} %eq.3), kind=kLoop, calls=%fused_computation.71 | loop fusion | flops 327680 | bytes 1966081 | tf_op jit(solution)/shard_map/jit(_where)/select_n | solution.py:48
  27.5 3.5 %collective-permute-start.1 = (bf16[4,128,8,80]{1,0,3,2:T(4,128)(2,1)}, bf16[4,128,8,80]{1,0,3,2:T(4,128)(2,1)}, u32[]{:S(2)}, u32[]{:S(2)}) collective-permute-start(bf16[4,128,8,80]{1,0,3,2:T(4,128)(2,1)} %copy_select_fusion.3), channel_id=1, source_target_pairs={{0,1},{1,2},{2,3},{3,4},{4,5},{5,6},{6,7},{7,8},{8,9},{9,10},{10,1... | collective-permute-start | bytes 1966088 | tf_op jit(solution)/shard_map/ppermute | solution.py:15
  31.1 2.2 %copy.84 = bf16[1,4,128,640]{2,3,1,0:T(8,128)(2,1)} copy(bf16[1,4,128,640]{3,2,1,0:T(8,128)(2,1)} %get-tuple-element.17) | data formatting | bytes 1310720
  33.2 3.9 %convolution_convert_fusion.3 = bf16[512,640]{1,0:T(8,128)(2,1)} fusion(bf16[1280,640]{1,0:T(8,128)(2,1)} %param.12, bf16[512,1280]{1,0:T(8,128)(2,1)} %copy-done.3, f32[1280]{0:T(1024)S(1)} %copy-done.6, f32[512]{0:T(512)S(1)} %add_rsqrt_fusion, f32[512]{0:T(512)S(1)} %broadcast_multiply_fusion), kind=kOutput, calls=%fused_computation.37 | convolution fusion | flops 842465280 | bytes 3613696 | tf_op jit(solution)/shard_map/dot_general | solution.py:29
  37.2 2.2 %copy.9 = bf16[512,640]{0,1:T(8,128)(2,1)} copy(bf16[512,640]{1,0:T(8,128)(2,1)} %convolution_convert_fusion.3) | data formatting | bytes 1310720 | tf_op jit(solution)/shard_map/convert_element_type | solution.py:30
  39.4 2.3 %reshape.109 = bf16[4,128,8,80]{1,0,3,2:T(4,128)(2,1)} reshape(bf16[512,640]{0,1:T(8,128)(2,1)} %copy.9) | data formatting | bytes 1310720 | tf_op jit(solution)/shard_map/reshape | solution.py:31
  41.7 1.1 %copy.85 = bf16[1,4,128,640]{2,3,1,0:T(8,128)(2,1)} copy(bf16[1,4,128,640]{3,2,1,0:T(8,128)(2,1)S(1)} %get-tuple-element.18) | data formatting | bytes 1310720
  43.1 2.0 %copy_select_fusion.1 = bf16[4,128,8,80]{1,0,3,2:T(4,128)(2,1)S(1)} fusion(bf16[4,128,8,80]{1,0,3,2:T(4,128)(2,1)} %collective-permute-done.2, bf16[4,128,8,80]{1,3,2,0:T(8,128)(2,1)} %bitcast.157, pred[]{:T(512)S(6)} %eq.3), kind=kLoop, calls=%fused_computation.69 | loop fusion | flops 327680 | bytes 1966081 | tf_op jit(solution)/shard_map/jit(_where)/select_n | solution.py:49
  45.2 2.2 %collective-permute-start.3 = (bf16[4,128,8,80]{1,0,3,2:T(4,128)(2,1)S(1)}, bf16[4,128,8,80]{1,0,3,2:T(4,128)(2,1)S(1)}, u32[]{:S(2)}, u32[]{:S(2)}) collective-permute-start(bf16[4,128,8,80]{1,0,3,2:T(4,128)(2,1)S(1)} %copy_select_fusion.1), channel_id=1, source_target_pairs={{0,1},{1,2},{2,3},{3,4},{4,5},{5,6},{6,7},{7,8},{8,9},{9,10},{10,1... | collective-permute-start | bytes 1966088 | tf_op jit(solution)/shard_map/ppermute | solution.py:15
  47.4 1.8 %copy_select_fusion.2 = bf16[4,128,8,80]{1,0,3,2:T(4,128)(2,1)S(1)} fusion(bf16[4,128,8,80]{1,0,3,2:T(4,128)(2,1)} %collective-permute-done.1, bf16[4,128,8,80]{1,3,2,0:T(8,128)(2,1)S(1)} %bitcast.155, pred[]{:T(512)S(6)} %eq.3), kind=kLoop, calls=%fused_computation.70 | loop fusion | flops 327680 | bytes 1966081 | tf_op jit(solution)/shard_map/jit(_where)/select_n | solution.py:51
  49.2 10.0 %fusion.13 = (f32[4,8,128]{2,0,1:T(4,128)S(1)}, f32[4,8,128]{2,0,1:T(4,128)S(1)}, f32[4,8,128]{2,0,1:T(4,128)S(1)}, f32[4,8,128]{2,0,1:T(4,128)S(1)}, f32[4,8,12...) fusion(bf16[4,128,8,80]{1,0,3,2:T(4,128)(2,1)} %copy_select_fus, ...), kind=kLoop, calls=%fused_computation.45 | loop fusion | flops 17002496 | bytes 2768896 | tf_op jit(solution)/shard_map/tphe,tphe->thp/dot_general | solution.py:61
  59.6 0.7 copy_select_fusion
  60.3 6.6 %add_convert_fusion = bf16[4,128,8,80]{1,0,3,2:T(4,128)(2,1)S(1)} fusion(bf16[4,128,8,80]{1,0,3,2:T(4,128)(2,1)S(1)} %copy_select_fusion, bf16[4,128,8,80]{1,0,3,2:T(4,128)(2,1)S(1)} %copy_select_fusion.1, bf16[4,128,8,80]{1,0,3,2:T(4,128)(2,1)} %reshape.112, f32[4,128,8]{1,0,2:T(4,128)S(1)} %get-tuple-element.22, f32[4,128,8]{1,0,2:T(4,128)S(1)} %get-tuple-element.23, ...), kind=kLoop, calls=%fused_computation.47 | loop fusion | flops 14745600 | bytes 2768896 | tf_op jit(solution)/shard_map/convert_element_type | solution.py:73
  66.9 2.3 %fusion.2 = bf16[512,1280]{1,0:T(8,128)(2,1)} fusion(bf16[640,1280]{1,0:T(8,128)(2,1)S(1)} %copy-done, bf16[512,1280]{1,0:T(8,128)(2,1)S(1)} %copy-done.4, bf16[80,8,4,128]{3,2,1,0:T(4,128)(2,1)S(1)} %bitcast.158), kind=kOutput, calls=%fused_computation.14 | convolution fusion | flops 840826880 | bytes 4915200 | tf_op jit(solution)/shard_map/dot_general | solution.py:74
  (36 shorter events, 1.7 us)
Async XLA Ops:
  0.0 66.9 %copy-start = (bf16[640,1280]{1,0:T(8,128)(2,1)S(1)}, bf16[640,1280]{1,0:T(8,128)(2,1)}, u32[]{:S(2)}) copy-start(bf16[640,1280]{1,0:T(8,128)(2,1)} %param.15) | copy-start | bytes 4915204
  0.0 6.1 %copy-start.5 = (bf16[1280,640]{1,0:T(8,128)(2,1)S(1)}, bf16[1280,640]{1,0:T(8,128)(2,1)}, u32[]{:S(2)}) copy-start(bf16[1280,640]{1,0:T(8,128)(2,1)} %param.13) | copy-start | bytes 4915204
  5.0 1.1 %copy-start.3 = (bf16[512,1280]{1,0:T(8,128)(2,1)}, bf16[512,1280]{1,0:T(8,128)(2,1)S(1)}, u32[]{:S(2)}) copy-start(bf16[512,1280]{1,0:T(8,128)(2,1)S(1)} %get-tuple-element.31) | copy-start | bytes 3932164
  5.0 1.1 %copy-start.6 = (f32[1280]{0:T(1024)S(1)}, f32[1280]{0:T(1024)}, u32[]{:S(2)}) copy-start(f32[1280]{0:T(1024)} %param.11) | copy-start | bytes 15364
  8.7 16.0 %collective-permute-start = (bf16[4,128,8,80]{1,0,3,2:T(4,128)(2,1)}, bf16[4,128,8,80]{1,0,3,2:T(4,128)(2,1)}, u32[]{:S(2)}, u32[]{:S(2)}) collective-permute-start(bf16[4,128,8,80]{1,0,3,2:T(4,128)(2,1)} %reshape.110), channel_id=1, source_target_pairs={{0,1},{1,2},{2,3},{3,4},{4,5},{5,6},{6,7},{7,8},{8,9},{9,10},{10,1... | collective-permute-start | bytes 1966088 | tf_op jit(solution)/shard_map/ppermute | solution.py:15
  17.6 25.6 %collective-permute-start.2 = (bf16[4,128,8,80]{1,0,3,2:T(4,128)(2,1)}, bf16[4,128,8,80]{1,0,3,2:T(4,128)(2,1)}, u32[]{:S(2)}, u32[]{:S(2)}) collective-permute-start(bf16[4,128,8,80]{1,0,3,2:T(4,128)(2,1)} %reshape.112), channel_id=1, source_target_pairs={{0,1},{1,2},{2,3},{3,4},{4,5},{5,6},{6,7},{7,8},{8,9},{9,10},{10,1... | collective-permute-start | bytes 1966088 | tf_op jit(solution)/shard_map/ppermute | solution.py:15
  27.5 19.9 %collective-permute-start.1 = (bf16[4,128,8,80]{1,0,3,2:T(4,128)(2,1)}, bf16[4,128,8,80]{1,0,3,2:T(4,128)(2,1)}, u32[]{:S(2)}, u32[]{:S(2)}) collective-permute-start(bf16[4,128,8,80]{1,0,3,2:T(4,128)(2,1)} %copy_select_fusion.3), channel_id=1, source_target_pairs={{0,1},{1,2},{2,3},{3,4},{4,5},{5,6},{6,7},{7,8},{8,9},{9,10},{10,1... | collective-permute-start | bytes 1966088 | tf_op jit(solution)/shard_map/ppermute | solution.py:15
  43.1 4.3 %copy-start.1 = (bf16[1,4,128,640]{2,3,1,0:T(8,128)(2,1)S(1)}, bf16[1,4,128,640]{2,3,1,0:T(8,128)(2,1)}, u32[]{:S(2)}) copy-start(bf16[1,4,128,640]{2,3,1,0:T(8,128)(2,1)} %copy.84) | copy-start | bytes 1966084
  45.1 4.1 %copy-start.2 = (bf16[4,128,8,80]{1,0,3,2:T(4,128)(2,1)S(1)}, bf16[4,128,8,80]{1,0,3,2:T(4,128)(2,1)}, u32[]{:S(2)}) copy-start(bf16[4,128,8,80]{1,0,3,2:T(4,128)(2,1)} %reshape.109) | copy-start | bytes 1966084
  45.2 14.5 %collective-permute-start.3 = (bf16[4,128,8,80]{1,0,3,2:T(4,128)(2,1)S(1)}, bf16[4,128,8,80]{1,0,3,2:T(4,128)(2,1)S(1)}, u32[]{:S(2)}, u32[]{:S(2)}) collective-permute-start(bf16[4,128,8,80]{1,0,3,2:T(4,128)(2,1)S(1)} %copy_select_fusion.1), channel_id=1, source_target_pairs={{0,1},{1,2},{2,3},{3,4},{4,5},{5,6},{6,7},{7,8},{8,9},{9,10},{10,1... | collective-permute-start | bytes 1966088 | tf_op jit(solution)/shard_map/ppermute | solution.py:15
  60.3 6.6 %copy-start.4 = (bf16[512,1280]{1,0:T(8,128)(2,1)S(1)}, bf16[512,1280]{1,0:T(8,128)(2,1)}, u32[]{:S(2)}) copy-start(bf16[512,1280]{1,0:T(8,128)(2,1)} %copy-done.3) | copy-start | bytes 3932164
where the time goes:
time: 69.9 us; the launch traced here: 69.2 us
  other arithmetic  24.7 us (35%)
  local copies, waits for them, and re-layouts  16.4 us (23%)
  matrix products  15.7 us (22%)
  starting transfers between devices  12.2 us (17%)
    ppermute x4, starting transfers between devices, shifted_2(): lax.ppermute(value, axis, [(source, source + steps) for source in range(f...  12.2 us
    dot_general x1, other arithmetic, body(): jnp.einsum('tphe,tphe->thp', query, shifted, preferred_element_type=jnp.f...  10 us
    convert_element_type x1, other arithmetic, body(): mixed = mixed.astype(jnp.bfloat16).reshape(tub * pat, HEADS * HEAD_DIM)  6.58 us
    unnamed x18, local copies, waits for them, and re-layouts  6.33 us
    dot_general x1, matrix products, body(): jnp.dot(flat, w_embed, preferred_element_type=jnp.float32)  5.01 us
    dot_general x1, matrix products, body(): jnp.dot(normed, w_query, preferred_element_type=jnp.float32)  3.94 us
    dot_general x1, matrix products, body(): jnp.dot(normed, w_value, preferred_element_type=jnp.float32)  3.1 us
    slice x1, local copies, waits for them, and re-layouts, body(): far_key = jnp.where(is_first, prior_key[:tub], far_raw[0])  3.08 us
  transfers between devices with their start and end apart: 4, of which 0 were waited for; matrix products, arithmetic and copies ran while one was open for 56% of the time, Pallas kernels for 0%

commit v1 on v0

v1 whole, which is shorter than its diff:
```python
import functools
import math

import jax
import jax.numpy as jnp
from jax import lax
from jax.experimental import pallas as pl
from jax.experimental.pallas import tpu as pltpu
from jax.sharding import PartitionSpec as P

HEADS = 8
HEAD_DIM = 80
LANE = 128
CHUNK = 16
GROUP = 2
MESH = pl.DeviceIdType.MESH


def kernel(
    pixels,
    prior,
    w_embed,
    ln_gain,
    w_query,
    w_key,
    w_value,
    w_out,
    encoded,
    pix,
    we,
    gain,
    wq,
    wk,
    wv,
    wo,
    emb,
    qry,
    kv,
    out,
    mask,
    w_sem,
    pix_sem,
    prior_sem,
    out_sem,
    far_send,
    far_recv,
    near_send,
    near_recv,
):
    count = lax.axis_size("tm")
    me = lax.axis_index("tm")
    tub = pixels.shape[0]
    chunks = pixels.shape[1] // CHUNK
    half = kv.shape[3] // 2
    width = emb.shape[3]
    rows = tub * CHUNK
    is_even = lax.rem(me, 2) == 0
    partner = jnp.where(is_even, me + 1, me - 1)
    has_before = me >= 2
    has_after = me + 2 < count

    barrier = pltpu.get_barrier_semaphore()
    pl.semaphore_signal(barrier, inc=1, device_id={"tm": partner}, device_id_type=MESH)

    @pl.when(has_before)
    def _():
        pl.semaphore_signal(barrier, inc=1, device_id={"tm": me - 2}, device_id_type=MESH)

    @pl.when(has_after)
    def _():
        pl.semaphore_signal(barrier, inc=1, device_id={"tm": me + 2}, device_id_type=MESH)

    def patches(c):
        return pl.ds(pl.multiple_of(c * CHUNK, CHUNK), CHUNK)

    def load_pix(c):
        return pltpu.make_async_copy(pixels.at[:, patches(c), :], pix.at[c], pix_sem.at[c])

    def load_weight(source, target, index):
        return pltpu.make_async_copy(source, target, w_sem.at[index])

    get_we = load_weight(w_embed, we, 0)
    get_gain = load_weight(ln_gain, gain, 1)
    get_wk = load_weight(w_key, wk, 2)
    get_wv = load_weight(w_value, wv, 3)
    get_wq = load_weight(w_query, wq, 4)
    get_wo = load_weight(w_out, wo, 5)

    def load_prior(c, which, first, slot, index):
        return pltpu.make_async_copy(
            prior.at[which, pl.ds(first, tub), patches(c), :],
            kv.at[c, pl.ds(slot, tub), :, pl.ds(which * half, half)],
            prior_sem.at[index, which, c],
        )

    def send_far(c):
        return pltpu.make_async_remote_copy(
            src_ref=kv.at[c, pl.ds(2 * tub, tub)],
            dst_ref=kv.at[c, pl.ds(0, tub)],
            send_sem=far_send.at[c],
            recv_sem=far_recv.at[c],
            device_id={"tm": me + 2},
            device_id_type=MESH,
        )

    def send_near(c, slot):
        return pltpu.make_async_remote_copy(
            src_ref=kv.at[c, pl.ds(slot, tub)],
            dst_ref=kv.at[c, pl.ds(tub, tub)],
            send_sem=near_send.at[c],
            recv_sem=near_recv.at[c],
            device_id={"tm": partner},
            device_id_type=MESH,
        )

    def store_out(c):
        return pltpu.make_async_copy(out.at[c], encoded.at[:, patches(c), :], out_sem.at[c])

    for c in range(GROUP):
        load_pix(c).start()
    get_we.start()
    get_gain.start()
    get_wk.start()
    get_wv.start()
    get_wq.start()
    for c in range(GROUP, chunks):
        load_pix(c).start()
    get_wo.start()

    @pl.when(me == 0)
    def _():
        def start(c, carry):
            for which in range(2):
                load_prior(c, which, 0, 0, 0).start()
                load_prior(c, which, tub, tub, 1).start()
            return carry

        lax.fori_loop(0, chunks, start, 0)

    @pl.when(me == 1)
    def _():
        def start(c, carry):
            for which in range(2):
                load_prior(c, which, tub, 0, 0).start()
            return carry

        lax.fori_loop(0, chunks, start, 0)

    total = 2 * rows
    keys = 3 * tub * CHUNK
    row = lax.broadcasted_iota(jnp.int32, (total, keys), 0)
    col = lax.broadcasted_iota(jnp.int32, (total, keys), 1)
    step_t = lax.rem(row, rows) // CHUNK
    step_s = col // CHUNK
    same = lax.rem(row, CHUNK) == lax.rem(col, CHUNK)
    valid = same & (step_s >= step_t) & (step_s <= step_t + 2 * tub)
    mask[...] = jnp.where(valid, 1.0, 0.0)

    def project(s, carry):
        first = s * GROUP
        for g in range(GROUP):
            load_pix(first + g).wait()

        @pl.when(s == 0)
        def _():
            get_we.wait()
            get_gain.wait()

        flat = pix[pl.ds(first, GROUP)].reshape(GROUP * rows, pix.shape[3])
        embedded = jnp.dot(flat, we[...], preferred_element_type=jnp.float32).astype(jnp.bfloat16)
        emb[pl.ds(first, GROUP)] = embedded.reshape(GROUP, tub, CHUNK, width)
        wide = embedded.astype(jnp.float32)
        center = wide - jnp.mean(wide, axis=-1, keepdims=True)
        spread = jnp.mean(center * center, axis=-1, keepdims=True)
        normed = (center * lax.rsqrt(spread + 1e-06) * gain[...]).astype(jnp.bfloat16)

        @pl.when(s == 0)
        def _():
            get_wk.wait()
            get_wv.wait()

        shape4 = (GROUP, tub, CHUNK, half)
        key = jnp.dot(normed, wk[...], preferred_element_type=jnp.float32).astype(jnp.bfloat16)
        kv[pl.ds(first, GROUP), pl.ds(2 * tub, tub), :, pl.ds(0, half)] = key.reshape(shape4)
        value = jnp.dot(normed, wv[...], preferred_element_type=jnp.float32).astype(jnp.bfloat16)
        kv[pl.ds(first, GROUP), pl.ds(2 * tub, tub), :, pl.ds(half, half)] = value.reshape(shape4)

        @pl.when(s == 0)
        def _():
            expected = 1 + has_before.astype(jnp.int32) + has_after.astype(jnp.int32)
            pl.semaphore_wait(barrier, expected)

        for g in range(GROUP):

            @pl.when(has_after)
            def _():
                send_far(first + g).start()

            @pl.when(is_even)
            def _():
                send_near(first + g, 2 * tub).start()

        @pl.when(s == 0)
        def _():
            get_wq.wait()

        query = jnp.dot(normed, wq[...], preferred_element_type=jnp.float32).astype(jnp.bfloat16)
        qry[pl.ds(first, GROUP)] = query.reshape(shape4)
        return carry

    lax.fori_loop(0, chunks // GROUP, project, 0)
    get_wo.wait()

    @pl.when(me == 0)
    def _():
        def finish(c, carry):
            for which in range(2):
                load_prior(c, which, 0, 0, 0).wait()
                load_prior(c, which, tub, tub, 1).wait()
            return carry

        lax.fori_loop(0, chunks, finish, 0)

    @pl.when(me == 1)
    def _():
        def finish(c, carry):
            for which in range(2):
                load_prior(c, which, tub, 0, 0).wait()
            return carry

        lax.fori_loop(0, chunks, finish, 0)

    scale = 1.0 / math.sqrt(HEAD_DIM)
    window = 2 * LANE
    lane = lax.broadcasted_iota(jnp.int32, (1, window), 1)

    def attend(c, carry):
        @pl.when(has_before)
        def _():
            send_far(c).wait_recv()

        @pl.when(has_before & jnp.logical_not(is_even))
        def _():
            send_near(c, 0).start()

        @pl.when(has_before | jnp.logical_not(is_even))
        def _():
            send_near(c, 0).wait_recv()

        tiles = [None] * (half // LANE)
        for pair in range(HEADS // 2):
            low = 2 * pair * HEAD_DIM
            base = low // LANE * LANE
            picks = []
            for head in range(2):
                begin = low + head * HEAD_DIM - base
                picks.append(jnp.where((lane >= begin) & (lane < begin + HEAD_DIM), 1.0, 0.0))
            q = qry[c, :, :, pl.ds(base, window)].reshape(rows, window)
            both = jnp.concatenate([q * pick.astype(jnp.bfloat16) for pick in picks], axis=0)
            k = kv[c, :, :, pl.ds(base, window)].reshape(keys, window)
            scores = lax.dot_general(
                both, k, (((1,), (1,)), ((), ())), preferred_element_type=jnp.float32
            )
            scores = jnp.where(mask[...] > 0.5, scores * scale, -jnp.inf)
            top = jnp.max(scores, axis=-1, keepdims=True)
            expo = jnp.exp(scores - top)
            weights = (expo / jnp.sum(expo, axis=-1, keepdims=True)).astype(jnp.bfloat16)
            v = kv[c, :, :, pl.ds(half + base, window)].reshape(keys, window)
            mixed = jnp.dot(weights, v, preferred_element_type=jnp.float32)
            part = mixed[:rows] * picks[0] + mixed[rows:] * picks[1]
            for side in range(2):
                piece = part[:, side * LANE : (side + 1) * LANE]
                at = base // LANE + side
                tiles[at] = piece if tiles[at] is None else tiles[at] + piece
        mixed = jnp.concatenate(tiles, axis=1).astype(jnp.bfloat16)
        result = emb[c].reshape(rows, width).astype(jnp.float32) + jnp.dot(
            mixed, wo[...], preferred_element_type=jnp.float32
        )
        out[c] = result.astype(jnp.bfloat16).reshape(tub, CHUNK, width)
        store_out(c).start()
        return carry

    lax.fori_loop(0, chunks, attend, 0)

    def drain(c, carry):
        store_out(c).wait()

        @pl.when(has_after)
        def _():
            send_far(c).wait_send()

        @pl.when(has_before | is_even)
        def _():
            send_near(c, 0).wait_send()

        return carry

    lax.fori_loop(0, chunks, drain, 0)


def body(pixels, prior_kv, w_embed, ln_gain, w_query, w_key, w_value, w_out):
    tub, pat, pix = pixels.shape
    width = w_embed.shape[1]
    half = w_key.shape[1]
    chunks = pat // CHUNK
    bf16 = jnp.bfloat16
    dma = pltpu.SemaphoreType.DMA
    return pl.pallas_call(
        kernel,
        out_shape=jax.ShapeDtypeStruct((tub, pat, width), bf16),
        in_specs=[pl.BlockSpec(memory_space=pl.ANY)] * 8,
        out_specs=pl.BlockSpec(memory_space=pl.ANY),
        scratch_shapes=[
            pltpu.VMEM((chunks, tub, CHUNK, pix), bf16),
            pltpu.VMEM(w_embed.shape, bf16),
            pltpu.VMEM((1, width), jnp.float32),
            pltpu.VMEM(w_query.shape, bf16),
            pltpu.VMEM(w_key.shape, bf16),
            pltpu.VMEM(w_value.shape, bf16),
            pltpu.VMEM(w_out.shape, bf16),
            pltpu.VMEM((chunks, tub, CHUNK, width), bf16),
            pltpu.VMEM((chunks, tub, CHUNK, half), bf16),
            pltpu.VMEM((chunks, 3 * tub, CHUNK, 2 * half), bf16),
            pltpu.VMEM((chunks, tub, CHUNK, width), bf16),
            pltpu.VMEM((2 * tub * CHUNK, 3 * tub * CHUNK), jnp.float32),
            dma((6,)),
            dma((chunks,)),
            dma((2, 2, chunks)),
            dma((chunks,)),
            dma((chunks,)),
            dma((chunks,)),
            dma((chunks,)),
            dma((chunks,)),
        ],
        compiler_params=pltpu.CompilerParams(collective_id=0, has_side_effects=True),
    )(pixels, prior_kv, w_embed, ln_gain.reshape(1, width), w_query, w_key, w_value, w_out)


def solution(mesh):
    placed = (
        P(("groups", "tm"), None, None),
        P(None, "groups", None, None),
        P(),
        P(),
        P(),
        P(),
        P(),
        P(),
    )
    return jax.shard_map(
        body, mesh=mesh, in_specs=placed, out_specs=P(("groups", "tm"), None, None), check_vma=False
    )
```

time: 69.9 us -> 41.6 us (0.60)
  the two profiles are of different devices: /device:TPU:1 before, /device:TPU:10 now
where the time goes in v1:
time: 41.6 us; the launch traced here: 41.4 us
  Pallas kernels  37.7 us (91%)
  local copies, waits for them, and re-layouts  3.75 us (9%)
    pallas_call x1, Pallas kernels, body(): pl.pallas_call(kernel, out_shape=jax.ShapeDtypeStruct((tub, pat, width),...  37.7 us
    unnamed x1, local copies, waits for them, and re-layouts  2.46 us
    reshape x1, local copies, waits for them, and re-layouts, body(): ln_gain.reshape(1, width)  1.29 us

profile of v1, /device:TPU:10, one launch (start us, length us, event | category | flops | bytes accessed | tf_op | source)
XLA Modules:
  0.0 41.4 jit_solution(8565353185712340825)
XLA Ops:
  0.0 1.3 %reshape.3.ln_gain = f32[1,1280]{1,0:T(1,128)} reshape(f32[1280]{0:T(1024)} %param.11) | data formatting | bytes 10240 | tf_op jit(solution)/shard_map/reshape | solution.py:336
  1.3 37.7 %shard_map.82 = bf16[4,128,1280]{2,1,0:T(8,128)(2,1)} custom-call(bf16[4,128,1536]{2,1,0:T(8,128)(2,1)} %pixels.1, bf16[2,8,128,640]{3,2,1,0:T(8,128)(2,1)} %prior.1, bf16[1536,1280]{1,0:T(8,128)(2,1)} %w_embed.1, f32[1,1280]{1,0:T(1,128)} %reshape.3.ln_gain, bf16[1280,640]{1,0:T(8,128)(2,1)} %w_query.1, bf16[1280,640]{1,0:T(8,128)(2,1)} %w_key.1, ...), custom_call_target="tpu_custom_call" | custom-call | tf_op jit(solution)/shard_map/pallas_call | solution.py:308
  39.0 2.5 %copy.10 = bf16[4,128,1280]{2,1,0:T(8,128)(2,1)} copy(bf16[4,128,1280]{2,1,0:T(8,128)(2,1)} %shard_map.82) | data formatting | bytes 2621440

commit v2 on v1

--- a/solution.py
+++ b/solution.py
@@ -27,6 +27,7 @@
     w_out,
     encoded,
     pix,
+    far_pix,
     we,
     gain,
     wq,
@@ -46,6 +47,8 @@
     far_recv,
     near_send,
     near_recv,
+    raw_send,
+    raw_recv,
 ):
     count = lax.axis_size("tm")
     me = lax.axis_index("tm")
@@ -55,8 +58,11 @@
     width = emb.shape[3]
     rows = tub * CHUNK
     is_even = lax.rem(me, 2) == 0
+    is_odd = jnp.logical_not(is_even)
     partner = jnp.where(is_even, me + 1, me - 1)
     has_before = me >= 2
+    steps = chunks // GROUP
+    turn = lax.rem(me, 2)
     has_after = me + 2 < count
 
     barrier = pltpu.get_barrier_semaphore()
@@ -103,6 +109,16 @@
             device_id_type=MESH,
         )
 
+    def send_raw(g):
+        return pltpu.make_async_remote_copy(
+            src_ref=pixels.at[:, patches(g), :],
+            dst_ref=far_pix.at[g],
+            send_sem=raw_send.at[g],
+            recv_sem=raw_recv.at[g],
+            device_id={"tm": me + 2},
+            device_id_type=MESH,
+        )
+
     def send_near(c, slot):
         return pltpu.make_async_remote_copy(
             src_ref=kv.at[c, pl.ds(slot, tub)],
@@ -116,15 +132,16 @@
     def store_out(c):
         return pltpu.make_async_copy(out.at[c], encoded.at[:, patches(c), :], out_sem.at[c])
 
-    for c in range(GROUP):
-        load_pix(c).start()
+    for g in range(GROUP):
+        load_pix(lax.rem(turn, steps) * GROUP + g).start()
     get_we.start()
     get_gain.start()
     get_wk.start()
     get_wv.start()
     get_wq.start()
-    for c in range(GROUP, chunks):
-        load_pix(c).start()
+    for s in range(1, steps):
+        for g in range(GROUP):
+            load_pix(lax.rem(s + turn, steps) * GROUP + g).start()
     get_wo.start()
 
     @pl.when(me == 0)
@@ -145,6 +162,14 @@
             return carry
 
         lax.fori_loop(0, chunks, start, 0)
+
+    expected = 1 + has_before.astype(jnp.int32) + has_after.astype(jnp.int32)
+    pl.semaphore_wait(barrier, expected)
+
+    @pl.when(has_after & is_odd)
+    def _():
+        for g in range(GROUP):
+            send_raw(g).start()
 
     total = 2 * rows
     keys = 3 * tub * CHUNK
@@ -156,43 +181,48 @@
     valid = same & (step_s >= step_t) & (step_s <= step_t + 2 * tub)
     mask[...] = jnp.where(valid, 1.0, 0.0)
 
-    def project(s, carry):
-        first = s * GROUP
-        for g in range(GROUP):
-            load_pix(first + g).wait()
-
-        @pl.when(s == 0)
-        def _():
-            get_we.wait()
-            get_gain.wait()
-
-        flat = pix[pl.ds(first, GROUP)].reshape(GROUP * rows, pix.shape[3])
+
+    def normalize(flat):
         embedded = jnp.dot(flat, we[...], preferred_element_type=jnp.float32).astype(jnp.bfloat16)
-        emb[pl.ds(first, GROUP)] = embedded.reshape(GROUP, tub, CHUNK, width)
         wide = embedded.astype(jnp.float32)
         center = wide - jnp.mean(wide, axis=-1, keepdims=True)
         spread = jnp.mean(center * center, axis=-1, keepdims=True)
-        normed = (center * lax.rsqrt(spread + 1e-06) * gain[...]).astype(jnp.bfloat16)
+        scaled = center * lax.rsqrt(spread + 1e-06) * gain[...].reshape(1, width)
+        return embedded, scaled.astype(jnp.bfloat16)
+
+    shape4 = (GROUP, tub, CHUNK, half)
+
+    def fill(normed, first, slot):
+        for weight, lane in ((wk, 0), (wv, half)):
+            part = jnp.dot(normed, weight[...], preferred_element_type=jnp.float32)
+            kv[pl.ds(first, GROUP), pl.ds(slot, tub), :, pl.ds(lane, half)] = part.astype(
+                jnp.bfloat16
+            ).reshape(shape4)
+
+    def project(s, carry):
+        first = lax.rem(s + turn, steps) * GROUP
+        for g in range(GROUP):
+            load_pix(first + g).wait()
+
+        @pl.when(s == 0)
+        def _():
+            get_we.wait()
+            get_gain.wait()
+
+        flat = pix[pl.ds(first, GROUP)].reshape(GROUP * rows, pix.shape[3])
+        embedded, normed = normalize(flat)
+        emb[pl.ds(first, GROUP)] = embedded.reshape(GROUP, tub, CHUNK, width)
 
         @pl.when(s == 0)
         def _():
             get_wk.wait()
             get_wv.wait()
 
-        shape4 = (GROUP, tub, CHUNK, half)
-        key = jnp.dot(normed, wk[...], preferred_element_type=jnp.float32).astype(jnp.bfloat16)
-        kv[pl.ds(first, GROUP), pl.ds(2 * tub, tub), :, pl.ds(0, half)] = key.reshape(shape4)
-        value = jnp.dot(normed, wv[...], preferred_element_type=jnp.float32).astype(jnp.bfloat16)
-        kv[pl.ds(first, GROUP), pl.ds(2 * tub, tub), :, pl.ds(half, half)] = value.reshape(shape4)
-
-        @pl.when(s == 0)
-        def _():
-            expected = 1 + has_before.astype(jnp.int32) + has_after.astype(jnp.int32)
-            pl.semaphore_wait(barrier, expected)
-
-        for g in range(GROUP):
-
-            @pl.when(has_after)
+        fill(normed, first, 2 * tub)
+
+        for g in range(GROUP):
+
+            @pl.when(has_after & (is_even | (first > 0)))
             def _():
                 send_far(first + g).start()
 
@@ -208,7 +238,15 @@
         qry[pl.ds(first, GROUP)] = query.reshape(shape4)
         return carry
 
-    lax.fori_loop(0, chunks // GROUP, project, 0)
+    lax.fori_loop(0, steps, project, 0)
+
+    @pl.when(has_before & is_odd)
+    def _():
+        for g in range(GROUP):
+            send_raw(g).wait_recv()
+        _, normed = normalize(far_pix[...].reshape(GROUP * rows, pix.shape[3]))
+        fill(normed, 0, 0)
+
     get_wo.wait()
 
     @pl.when(me == 0)
@@ -235,15 +273,15 @@
     lane = lax.broadcasted_iota(jnp.int32, (1, window), 1)
 
     def attend(c, carry):
-        @pl.when(has_before)
+        @pl.when(has_before & (is_even | (c >= GROUP)))
         def _():
             send_far(c).wait_recv()
 
-        @pl.when(has_before & jnp.logical_not(is_even))
+        @pl.when(has_before & is_odd)
         def _():
             send_near(c, 0).start()
 
-        @pl.when(has_before | jnp.logical_not(is_even))
+        @pl.when(has_before | is_odd)
         def _():
             send_near(c, 0).wait_recv()
 
@@ -285,7 +323,7 @@
     def drain(c, carry):
         store_out(c).wait()
 
-        @pl.when(has_after)
+        @pl.when(has_after & (is_even | (c >= GROUP)))
         def _():
             send_far(c).wait_send()
 
@@ -296,6 +334,11 @@
         return carry
 
     lax.fori_loop(0, chunks, drain, 0)
+
+    @pl.when(has_after & is_odd)
+    def _():
+        for g in range(GROUP):
+            send_raw(g).wait_send()
 
 
 def body(pixels, prior_kv, w_embed, ln_gain, w_query, w_key, w_value, w_out):
@@ -312,8 +355,9 @@
         out_specs=pl.BlockSpec(memory_space=pl.ANY),
         scratch_shapes=[
             pltpu.VMEM((chunks, tub, CHUNK, pix), bf16),
+            pltpu.VMEM((GROUP, tub, CHUNK, pix), bf16),
             pltpu.VMEM(w_embed.shape, bf16),
-            pltpu.VMEM((1, width), jnp.float32),
+            pltpu.VMEM((width,), jnp.float32),
             pltpu.VMEM(w_query.shape, bf16),
             pltpu.VMEM(w_key.shape, bf16),
             pltpu.VMEM(w_value.shape, bf16),
@@ -331,9 +375,11 @@
             dma((chunks,)),
             dma((chunks,)),
             dma((chunks,)),
+            dma((GROUP,)),
+            dma((GROUP,)),
         ],
         compiler_params=pltpu.CompilerParams(collective_id=0, has_side_effects=True),
-    )(pixels, prior_kv, w_embed, ln_gain.reshape(1, width), w_query, w_key, w_value, w_out)
+    )(pixels, prior_kv, w_embed, ln_gain, w_query, w_key, w_value, w_out)
 
 
 def solution(mesh):

time: 41.6 us -> 38 us (0.913)
  Pallas kernels: 37.7 us -> 35.4 us
  local copies, waits for them, and re-layouts: 3.75 us -> 2.46 us
    pallas_call x1, Pallas kernels: 37.7 us -> 35.4 us  [body(): pl.pallas_call(kernel, out_shape=jax.ShapeDtypeStruct((tub, pat, width),...]
    reshape x1 -> x0, local copies, waits for them, and re-layouts: 1.29 us -> none  [body(): ln_gain.reshape(1, width)]
where the time goes in v2:
time: 38 us; the launch traced here: 37.9 us
  Pallas kernels  35.4 us (93%)
  local copies, waits for them, and re-layouts  2.46 us (6%)
    pallas_call x1, Pallas kernels, body(): pl.pallas_call(kernel, out_shape=jax.ShapeDtypeStruct((tub, pat, width),...  35.4 us
    unnamed x1, local copies, waits for them, and re-layouts  2.46 us

profile of v2, /device:TPU:10, one launch (start us, length us, event | category | flops | bytes accessed | tf_op | source)
XLA Modules:
  0.0 37.9 jit_solution(16102368859710607461)
XLA Ops:
  0.0 35.4 %shard_map.82 = bf16[4,128,1280]{2,1,0:T(8,128)(2,1)} custom-call(bf16[4,128,1536]{2,1,0:T(8,128)(2,1)} %pixels.1, bf16[2,8,128,640]{3,2,1,0:T(8,128)(2,1)} %prior.1, bf16[1536,1280]{1,0:T(8,128)(2,1)} %w_embed.1, f32[1280]{0:T(1024)} %ln_gain.1, bf16[1280,640]{1,0:T(8,128)(2,1)} %w_query.1, bf16[1280,640]{1,0:T(8,128)(2,1)} %w_key.1, ...), custom_call_target="tpu_custom_call" | custom-call | tf_op jit(solution)/shard_map/pallas_call | solution.py:351
  35.4 2.5 %copy.10 = bf16[4,128,1280]{2,1,0:T(8,128)(2,1)} copy(bf16[4,128,1280]{2,1,0:T(8,128)(2,1)} %shard_map.82) | data formatting | bytes 2621440

commit v3 on v2

--- a/solution.py
+++ b/solution.py
@@ -37,12 +37,10 @@
     emb,
     qry,
     kv,
-    out,
     mask,
     w_sem,
     pix_sem,
     prior_sem,
-    out_sem,
     far_send,
     far_recv,
     near_send,
@@ -128,9 +126,6 @@
             device_id={"tm": partner},
             device_id_type=MESH,
         )
-
-    def store_out(c):
-        return pltpu.make_async_copy(out.at[c], encoded.at[:, patches(c), :], out_sem.at[c])
 
     for g in range(GROUP):
         load_pix(lax.rem(turn, steps) * GROUP + g).start()
@@ -314,15 +309,12 @@
         result = emb[c].reshape(rows, width).astype(jnp.float32) + jnp.dot(
             mixed, wo[...], preferred_element_type=jnp.float32
         )
-        out[c] = result.astype(jnp.bfloat16).reshape(tub, CHUNK, width)
-        store_out(c).start()
+        encoded[:, patches(c), :] = result.astype(jnp.bfloat16).reshape(tub, CHUNK, width)
         return carry
 
     lax.fori_loop(0, chunks, attend, 0)
 
     def drain(c, carry):
-        store_out(c).wait()
-
         @pl.when(has_after & (is_even | (c >= GROUP)))
         def _():
             send_far(c).wait_send()
@@ -350,9 +342,9 @@
     dma = pltpu.SemaphoreType.DMA
     return pl.pallas_call(
         kernel,
-        out_shape=jax.ShapeDtypeStruct((tub, pat, width), bf16),
+        out_shape=pltpu.VMEM((tub, pat, width), bf16),
         in_specs=[pl.BlockSpec(memory_space=pl.ANY)] * 8,
-        out_specs=pl.BlockSpec(memory_space=pl.ANY),
+        out_specs=pl.BlockSpec(memory_space=pltpu.VMEM),
         scratch_shapes=[
             pltpu.VMEM((chunks, tub, CHUNK, pix), bf16),
             pltpu.VMEM((GROUP, tub, CHUNK, pix), bf16),
@@ -365,12 +357,10 @@
             pltpu.VMEM((chunks, tub, CHUNK, width), bf16),
             pltpu.VMEM((chunks, tub, CHUNK, half), bf16),
             pltpu.VMEM((chunks, 3 * tub, CHUNK, 2 * half), bf16),
-            pltpu.VMEM((chunks, tub, CHUNK, width), bf16),
             pltpu.VMEM((2 * tub * CHUNK, 3 * tub * CHUNK), jnp.float32),
             dma((6,)),
             dma((chunks,)),
             dma((2, 2, chunks)),
-            dma((chunks,)),
             dma((chunks,)),
             dma((chunks,)),
             dma((chunks,)),
@@ -378,7 +368,7 @@
             dma((GROUP,)),
             dma((GROUP,)),
         ],
-        compiler_params=pltpu.CompilerParams(collective_id=0, has_side_effects=True),
+        compiler_params=pltpu.CompilerParams(collective_id=0, has_side_effects=True, vmem_limit_bytes=65500000),
     )(pixels, prior_kv, w_embed, ln_gain, w_query, w_key, w_value, w_out)
 
 

time: 38 us -> 36 us (0.947)
  local copies, waits for them, and re-layouts: 2.46 us -> 1.06 us
  Pallas kernels: 35.4 us -> 34.7 us
    unnamed x1, local copies, waits for them, and re-layouts: 2.46 us -> 1.06 us
    pallas_call x1, Pallas kernels: 35.4 us -> 34.7 us  [body(): pl.pallas_call(kernel, out_shape=pltpu.VMEM((tub, pat, width), bf16), in_...]
where the time goes in v3:
time: 36 us; the launch traced here: 35.8 us
  Pallas kernels  34.7 us (96%)
  local copies, waits for them, and re-layouts  1.06 us (3%)
    pallas_call x1, Pallas kernels, body(): pl.pallas_call(kernel, out_shape=pltpu.VMEM((tub, pat, width), bf16), in_...  34.7 us
    unnamed x1, local copies, waits for them, and re-layouts  1.06 us

profile of v3, /device:TPU:10, one launch (start us, length us, event | category | flops | bytes accessed | tf_op | source)
XLA Modules:
  0.0 35.8 jit_solution(10663956046734173271)
XLA Ops:
  0.0 34.7 %shard_map.82 = bf16[4,128,1280]{2,1,0:T(8,128)(2,1)S(1)} custom-call(bf16[4,128,1536]{2,1,0:T(8,128)(2,1)} %pixels.1, bf16[2,8,128,640]{3,2,1,0:T(8,128)(2,1)} %prior.1, bf16[1536,1280]{1,0:T(8,128)(2,1)} %w_embed.1, f32[1280]{0:T(1024)} %ln_gain.1, bf16[1280,640]{1,0:T(8,128)(2,1)} %w_query.1, bf16[1280,640]{1,0:T(8,128)(2,1)} %w_key.1, ...), custom_call_target="tpu_custom_call" | custom-call | tf_op jit(solution)/shard_map/pallas_call | solution.py:343
  34.8 1.1 %copy.10 = bf16[4,128,1280]{2,1,0:T(8,128)(2,1)} copy(bf16[4,128,1280]{2,1,0:T(8,128)(2,1)S(1)} %shard_map.82) | data formatting | bytes 2621440

commit v4 on v3

--- a/solution.py
+++ b/solution.py
@@ -55,6 +55,7 @@
     half = kv.shape[3] // 2
     width = emb.shape[3]
     rows = tub * CHUNK
+    near, own, far = 0, tub, 2 * tub
     is_even = lax.rem(me, 2) == 0
     is_odd = jnp.logical_not(is_even)
     partner = jnp.where(is_even, me + 1, me - 1)
@@ -97,12 +98,13 @@
             prior_sem.at[index, which, c],
         )
 
-    def send_far(c):
+    def send_far(c, which):
+        lanes = pl.ds(which * half, half)
         return pltpu.make_async_remote_copy(
-            src_ref=kv.at[c, pl.ds(2 * tub, tub)],
-            dst_ref=kv.at[c, pl.ds(0, tub)],
-            send_sem=far_send.at[c],
-            recv_sem=far_recv.at[c],
+            src_ref=kv.at[c, pl.ds(own, tub), :, lanes],
+            dst_ref=kv.at[c, pl.ds(far, tub), :, lanes],
+            send_sem=far_send.at[which, c],
+            recv_sem=far_recv.at[which, c],
             device_id={"tm": me + 2},
             device_id_type=MESH,
         )
@@ -120,7 +122,7 @@
     def send_near(c, slot):
         return pltpu.make_async_remote_copy(
             src_ref=kv.at[c, pl.ds(slot, tub)],
-            dst_ref=kv.at[c, pl.ds(tub, tub)],
+            dst_ref=kv.at[c, pl.ds(near, tub)],
             send_sem=near_send.at[c],
             recv_sem=near_recv.at[c],
             device_id={"tm": partner},
@@ -143,8 +145,8 @@
     def _():
         def start(c, carry):
             for which in range(2):
-                load_prior(c, which, 0, 0, 0).start()
-                load_prior(c, which, tub, tub, 1).start()
+                load_prior(c, which, 0, far, 0).start()
+                load_prior(c, which, tub, near, 1).start()
             return carry
 
         lax.fori_loop(0, chunks, start, 0)
@@ -153,7 +155,7 @@
     def _():
         def start(c, carry):
             for which in range(2):
-                load_prior(c, which, tub, 0, 0).start()
+                load_prior(c, which, tub, far, 0).start()
             return carry
 
         lax.fori_loop(0, chunks, start, 0)
@@ -171,7 +173,8 @@
     row = lax.broadcasted_iota(jnp.int32, (total, keys), 0)
     col = lax.broadcasted_iota(jnp.int32, (total, keys), 1)
     step_t = lax.rem(row, rows) // CHUNK
-    step_s = col // CHUNK
+    slot = col // CHUNK
+    step_s = lax.rem(slot + tub, 3 * tub)
     same = lax.rem(row, CHUNK) == lax.rem(col, CHUNK)
     valid = same & (step_s >= step_t) & (step_s <= step_t + 2 * tub)
     mask[...] = jnp.where(valid, 1.0, 0.0)
@@ -213,17 +216,18 @@
             get_wk.wait()
             get_wv.wait()
 
-        fill(normed, first, 2 * tub)
+        fill(normed, first, own)
 
         for g in range(GROUP):
 
             @pl.when(has_after & (is_even | (first > 0)))
             def _():
-                send_far(first + g).start()
+                send_far(first + g, 0).start()
+                send_far(first + g, 1).start()
 
             @pl.when(is_even)
             def _():
-                send_near(first + g, 2 * tub).start()
+                send_near(first + g, own).start()
 
         @pl.when(s == 0)
         def _():
@@ -240,7 +244,7 @@
         for g in range(GROUP):
             send_raw(g).wait_recv()
         _, normed = normalize(far_pix[...].reshape(GROUP * rows, pix.shape[3]))
-        fill(normed, 0, 0)
+        fill(normed, 0, far)
 
     get_wo.wait()
 
@@ -248,8 +252,8 @@
     def _():
         def finish(c, carry):
             for which in range(2):
-                load_prior(c, which, 0, 0, 0).wait()
-                load_prior(c, which, tub, tub, 1).wait()
+                load_prior(c, which, 0, far, 0).wait()
+                load_prior(c, which, tub, near, 1).wait()
             return carry
 
         lax.fori_loop(0, chunks, finish, 0)
@@ -258,7 +262,7 @@
     def _():
         def finish(c, carry):
             for which in range(2):
-                load_prior(c, which, tub, 0, 0).wait()
+                load_prior(c, which, tub, far, 0).wait()
             return carry
 
         lax.fori_loop(0, chunks, finish, 0)
@@ -268,39 +272,71 @@
     lane = lax.broadcasted_iota(jnp.int32, (1, window), 1)
 
     def attend(c, carry):
-        @pl.when(has_before & (is_even | (c >= GROUP)))
-        def _():
-            send_far(c).wait_recv()
+        @pl.when(has_before & is_odd & (c >= GROUP))
+        def _():
+            send_far(c, 0).wait_recv()
+            send_far(c, 1).wait_recv()
 
         @pl.when(has_before & is_odd)
         def _():
-            send_near(c, 0).start()
+            send_near(c, far).start()
 
         @pl.when(has_before | is_odd)
         def _():
-            send_near(c, 0).wait_recv()
-
-        tiles = [None] * (half // LANE)
+            send_near(c, far).wait_recv()
+
+        def score(both, base, slot, size):
+            k = kv[c, pl.ds(slot, size), :, pl.ds(base, window)].reshape(size * CHUNK, window)
+            found = lax.dot_general(
+                both, k, (((1,), (1,)), ((), ())), preferred_element_type=jnp.float32
+            )
+            seen = mask[:, slot * CHUNK : (slot + size) * CHUNK] > 0.5
+            return jnp.where(seen, found * scale, -jnp.inf)
+
+        def blend(weights, base, slot, size):
+            v = kv[c, pl.ds(slot, size), :, pl.ds(half + base, window)]
+            return jnp.dot(
+                weights, v.reshape(size * CHUNK, window), preferred_element_type=jnp.float32
+            )
+
+        bases, picks, queries, early = [], [], [], []
         for pair in range(HEADS // 2):
             low = 2 * pair * HEAD_DIM
             base = low // LANE * LANE
-            picks = []
-            for head in range(2):
-                begin = low + head * HEAD_DIM - base
-                picks.append(jnp.where((lane >= begin) & (lane < begin + HEAD_DIM), 1.0, 0.0))
+            begins = [low + head * HEAD_DIM - base for head in range(2)]
+            pick = [
+                jnp.where((lane >= begin) & (lane < begin + HEAD_DIM), 1.0, 0.0) for begin in begins
+            ]
             q = qry[c, :, :, pl.ds(base, window)].reshape(rows, window)
-            both = jnp.concatenate([q * pick.astype(jnp.bfloat16) for pick in picks], axis=0)
-            k = kv[c, :, :, pl.ds(base, window)].reshape(keys, window)
-            scores = lax.dot_general(
-                both, k, (((1,), (1,)), ((), ())), preferred_element_type=jnp.float32
+            both = jnp.concatenate([q * one.astype(jnp.bfloat16) for one in pick], axis=0)
+            bases.append(base)
+            picks.append(pick)
+            queries.append(both)
+            early.append(score(both, base, near, 2 * tub))
+
+        @pl.when(has_before & is_even)
+        def _():
+            send_far(c, 0).wait_recv()
+
+        late, sums = [], []
+        for base, both, first in zip(bases, queries, early):
+            last = score(both, base, far, tub)
+            top = jnp.maximum(
+                jnp.max(first, axis=-1, keepdims=True), jnp.max(last, axis=-1, keepdims=True)
             )
-            scores = jnp.where(mask[...] > 0.5, scores * scale, -jnp.inf)
-            top = jnp.max(scores, axis=-1, keepdims=True)
-            expo = jnp.exp(scores - top)
-            weights = (expo / jnp.sum(expo, axis=-1, keepdims=True)).astype(jnp.bfloat16)
-            v = kv[c, :, :, pl.ds(half + base, window)].reshape(keys, window)
-            mixed = jnp.dot(weights, v, preferred_element_type=jnp.float32)
-            part = mixed[:rows] * picks[0] + mixed[rows:] * picks[1]
+            first, last = jnp.exp(first - top), jnp.exp(last - top)
+            weight = jnp.sum(first, axis=-1, keepdims=True) + jnp.sum(last, axis=-1, keepdims=True)
+            late.append((last / weight).astype(jnp.bfloat16))
+            sums.append(blend((first / weight).astype(jnp.bfloat16), base, near, 2 * tub))
+
+        @pl.when(has_before & is_even)
+        def _():
+            send_far(c, 1).wait_recv()
+
+        tiles = [None] * (half // LANE)
+        for base, pick, weights, mixed in zip(bases, picks, late, sums):
+            mixed = mixed + blend(weights, base, far, tub)
+            part = mixed[:rows] * pick[0] + mixed[rows:] * pick[1]
             for side in range(2):
                 piece = part[:, side * LANE : (side + 1) * LANE]
                 at = base // LANE + side
@@ -317,11 +353,12 @@
     def drain(c, carry):
         @pl.when(has_after & (is_even | (c >= GROUP)))
         def _():
-            send_far(c).wait_send()
+            send_far(c, 0).wait_send()
+            send_far(c, 1).wait_send()
 
         @pl.when(has_before | is_even)
         def _():
-            send_near(c, 0).wait_send()
+            send_near(c, far).wait_send()
 
         return carry
 
@@ -361,8 +398,8 @@
             dma((6,)),
             dma((chunks,)),
             dma((2, 2, chunks)),
-            dma((chunks,)),
-            dma((chunks,)),
+            dma((2, chunks)),
+            dma((2, chunks)),
             dma((chunks,)),
             dma((chunks,)),
             dma((GROUP,)),

time: 36 us -> 35.1 us (0.975)
  Pallas kernels: 34.7 us -> 33.9 us
    pallas_call x1, Pallas kernels: 34.7 us -> 33.9 us  [body(): pl.pallas_call(kernel, out_shape=pltpu.VMEM((tub, pat, width), bf16), in_...]
where the time goes in v4:
time: 35.1 us; the launch traced here: 35 us
  Pallas kernels  33.9 us (97%)
  local copies, waits for them, and re-layouts  1.06 us (3%)
    pallas_call x1, Pallas kernels, body(): pl.pallas_call(kernel, out_shape=pltpu.VMEM((tub, pat, width), bf16), in_...  33.9 us
    unnamed x1, local copies, waits for them, and re-layouts  1.06 us

profile of v4, /device:TPU:10, one launch (start us, length us, event | category | flops | bytes accessed | tf_op | source)
XLA Modules:
  0.0 35.0 jit_solution(12533747011973776855)
XLA Ops:
  0.0 33.9 %shard_map.82 = bf16[4,128,1280]{2,1,0:T(8,128)(2,1)S(1)} custom-call(bf16[4,128,1536]{2,1,0:T(8,128)(2,1)} %pixels.1, bf16[2,8,128,640]{3,2,1,0:T(8,128)(2,1)} %prior.1, bf16[1536,1280]{1,0:T(8,128)(2,1)} %w_embed.1, f32[1280]{0:T(1024)} %ln_gain.1, bf16[1280,640]{1,0:T(8,128)(2,1)} %w_query.1, bf16[1280,640]{1,0:T(8,128)(2,1)} %w_key.1, ...), custom_call_target="tpu_custom_call" | custom-call | tf_op jit(solution)/shard_map/pallas_call | solution.py:380
  33.9 1.1 %copy.10 = bf16[4,128,1280]{2,1,0:T(8,128)(2,1)} copy(bf16[4,128,1280]{2,1,0:T(8,128)(2,1)S(1)} %shard_map.82) | data formatting | bytes 2621440

commit v5 on v4

--- a/solution.py
+++ b/solution.py
@@ -168,6 +168,64 @@
         for g in range(GROUP):
             send_raw(g).start()
 
+    def normalize(flat):
+        embedded = jnp.dot(flat, we[...], preferred_element_type=jnp.float32).astype(jnp.bfloat16)
+        wide = embedded.astype(jnp.float32)
+        center = wide - jnp.mean(wide, axis=-1, keepdims=True)
+        spread = jnp.mean(center * center, axis=-1, keepdims=True)
+        scaled = center * lax.rsqrt(spread + 1e-06) * gain[...].reshape(1, width)
+        return embedded, scaled.astype(jnp.bfloat16)
+
+    shape4 = (GROUP, tub, CHUNK, half)
+
+    def fill(normed, first, slot):
+        for weight, lane in ((wk, 0), (wv, half)):
+            part = jnp.dot(normed, weight[...], preferred_element_type=jnp.float32)
+            kv[pl.ds(first, GROUP), pl.ds(slot, tub), :, pl.ds(lane, half)] = part.astype(
+                jnp.bfloat16
+            ).reshape(shape4)
+
+    def project(s, carry):
+        first = lax.rem(s + turn, steps) * GROUP
+        for g in range(GROUP):
+            load_pix(first + g).wait()
+
+        @pl.when(s == 0)
+        def _():
+            get_we.wait()
+            get_gain.wait()
+
+        flat = pix[pl.ds(first, GROUP)].reshape(GROUP * rows, pix.shape[3])
+        embedded, normed = normalize(flat)
+        emb[pl.ds(first, GROUP)] = embedded.reshape(GROUP, tub, CHUNK, width)
+
+        @pl.when(s == 0)
+        def _():
+            get_wk.wait()
+            get_wv.wait()
+
+        fill(normed, first, own)
+
+        for g in range(GROUP):
+
+            @pl.when(has_after & (is_even | (first > 0)))
+            def _():
+                send_far(first + g, 0).start()
+                send_far(first + g, 1).start()
+
+            @pl.when(is_even)
+            def _():
+                send_near(first + g, own).start()
+
+        @pl.when(s == 0)
+        def _():
+            get_wq.wait()
+
+        query = jnp.dot(normed, wq[...], preferred_element_type=jnp.float32).astype(jnp.bfloat16)
+        qry[pl.ds(first, GROUP)] = query.reshape(shape4)
+        return carry
+
+    lax.fori_loop(0, steps, project, 0)
     total = 2 * rows
     keys = 3 * tub * CHUNK
     row = lax.broadcasted_iota(jnp.int32, (total, keys), 0)
@@ -179,65 +237,6 @@
     valid = same & (step_s >= step_t) & (step_s <= step_t + 2 * tub)
     mask[...] = jnp.where(valid, 1.0, 0.0)
 
-
-    def normalize(flat):
-        embedded = jnp.dot(flat, we[...], preferred_element_type=jnp.float32).astype(jnp.bfloat16)
-        wide = embedded.astype(jnp.float32)
-        center = wide - jnp.mean(wide, axis=-1, keepdims=True)
-        spread = jnp.mean(center * center, axis=-1, keepdims=True)
-        scaled = center * lax.rsqrt(spread + 1e-06) * gain[...].reshape(1, width)
-        return embedded, scaled.astype(jnp.bfloat16)
-
-    shape4 = (GROUP, tub, CHUNK, half)
-
-    def fill(normed, first, slot):
-        for weight, lane in ((wk, 0), (wv, half)):
-            part = jnp.dot(normed, weight[...], preferred_element_type=jnp.float32)
-            kv[pl.ds(first, GROUP), pl.ds(slot, tub), :, pl.ds(lane, half)] = part.astype(
-                jnp.bfloat16
-            ).reshape(shape4)
-
-    def project(s, carry):
-        first = lax.rem(s + turn, steps) * GROUP
-        for g in range(GROUP):
-            load_pix(first + g).wait()
-
-        @pl.when(s == 0)
-        def _():
-            get_we.wait()
-            get_gain.wait()
-
-        flat = pix[pl.ds(first, GROUP)].reshape(GROUP * rows, pix.shape[3])
-        embedded, normed = normalize(flat)
-        emb[pl.ds(first, GROUP)] = embedded.reshape(GROUP, tub, CHUNK, width)
-
-        @pl.when(s == 0)
-        def _():
-            get_wk.wait()
-            get_wv.wait()
-
-        fill(normed, first, own)
-
-        for g in range(GROUP):
-
-            @pl.when(has_after & (is_even | (first > 0)))
-            def _():
-                send_far(first + g, 0).start()
-                send_far(first + g, 1).start()
-
-            @pl.when(is_even)
-            def _():
-                send_near(first + g, own).start()
-
-        @pl.when(s == 0)
-        def _():
-            get_wq.wait()
-
-        query = jnp.dot(normed, wq[...], preferred_element_type=jnp.float32).astype(jnp.bfloat16)
-        qry[pl.ds(first, GROUP)] = query.reshape(shape4)
-        return carry
-
-    lax.fori_loop(0, steps, project, 0)
 
     @pl.when(has_before & is_odd)
     def _():

time: 35.1 us -> 35.1 us (level)
  no operation moved by 1% of the time
where the time goes in v5:
time: 35.1 us; the launch traced here: 35 us
  Pallas kernels  33.9 us (97%)
  local copies, waits for them, and re-layouts  1.06 us (3%)
    pallas_call x1, Pallas kernels, body(): pl.pallas_call(kernel, out_shape=pltpu.VMEM((tub, pat, width), bf16), in_...  33.9 us
    unnamed x1, local copies, waits for them, and re-layouts  1.06 us

profile of v5, /device:TPU:10, one launch (start us, length us, event | category | flops | bytes accessed | tf_op | source)
XLA Modules:
  0.0 35.0 jit_solution(13607830161725985736)
XLA Ops:
  0.0 33.9 %shard_map.82 = bf16[4,128,1280]{2,1,0:T(8,128)(2,1)S(1)} custom-call(bf16[4,128,1536]{2,1,0:T(8,128)(2,1)} %pixels.1, bf16[2,8,128,640]{3,2,1,0:T(8,128)(2,1)} %prior.1, bf16[1536,1280]{1,0:T(8,128)(2,1)} %w_embed.1, f32[1280]{0:T(1024)} %ln_gain.1, bf16[1280,640]{1,0:T(8,128)(2,1)} %w_query.1, bf16[1280,640]{1,0:T(8,128)(2,1)} %w_key.1, ...), custom_call_target="tpu_custom_call" | custom-call | tf_op jit(solution)/shard_map/pallas_call | solution.py:379
  33.9 1.1 %copy.10 = bf16[4,128,1280]{2,1,0:T(8,128)(2,1)} copy(bf16[4,128,1280]{2,1,0:T(8,128)(2,1)S(1)} %shard_map.82) | data formatting | bytes 2621440
